TPU v7x, 32 devices: a whole 2x2x4 slice. The times are simulated.
32 devices in a mesh: blk: 4 (over x, core), ulysses: 8 (over z, y).
Axes of the slice: x: 2, y: 2, z: 4, core: 2. Of those that a mesh axis runs over, the one named last changes fastest.
Arguments:
- query_rows: bfloat16 [32, 4096, 128], P(None, ('blk', 'ulysses')), may hold values from -160 to 160
- out_grad: bfloat16 [32, 4096, 128], P(None, ('blk', 'ulysses')), may hold values from -6 to 6
- key_rows: bfloat16 [32, 512, 128], P(None, 'blk'), may hold values from -6 to 6
- value_rows: bfloat16 [32, 512, 128], P(None, 'blk'), may hold values from -6 to 6
- routes: int32 [4, 4], replicated, may hold values from 0 to 7
Outputs:
- query_grad: bfloat16 [32, 4096, 128], P(None, ('blk', 'ulysses'))
- key_grad: float32 [32, 512, 128], P(None, ('blk', 'ulysses'))
- value_grad: float32 [32, 512, 128], P(None, ('blk', 'ulysses'))
All inputs are finite; a program needn't handle non-finite values.
Results may differ from a plain program's by a relative error of at most 0.0056.
Values may be sent and summed in bfloat16 or wider, within the bound.
No kernel may reach another device: no remote copies, remote signals or barrier semaphores. Data moves between devices by JAX's collectives and lax.ppermute only.
A program may use at most 64 MiB of HBM per device.

v0:
```python
import math

import jax
import jax.numpy as jnp
from jax import lax
from jax.sharding import PartitionSpec as P

KB = 16


def body(query_rows, out_grad, key_rows, value_rows, routes):
    head_count, token_count, head_dim = query_rows.shape
    group_keys = key_rows.shape[1]
    cycle_size = lax.axis_size("blk")
    group_size = lax.axis_size("ulysses")
    sub_count = max(1, group_size // head_count)
    item_count = head_count * sub_count // group_size
    sub_length = token_count // sub_count
    row_count = group_size * sub_length
    block_count = group_keys // KB
    key_stride = token_count * group_size // group_keys
    score_scale = 1.0 / math.sqrt(head_dim)
    my_group = lax.axis_index("blk")
    my_rank = lax.axis_index("ulysses")
    packed_query = query_rows.reshape(head_count * sub_count, sub_length, head_dim)
    packed_grad = out_grad.reshape(head_count * sub_count, sub_length, head_dim)
    local_query, local_grad = (
        lax.all_to_all(packed_query, "ulysses", split_axis=0, concat_axis=1, tiled=True),
        lax.all_to_all(packed_grad, "ulysses", split_axis=0, concat_axis=1, tiled=True),
    )
    first_head = my_rank * item_count // sub_count
    own_keys = lax.dynamic_slice_in_dim(key_rows, first_head, item_count, 0)
    own_values = lax.dynamic_slice_in_dim(value_rows, first_head, item_count, 0)
    requested = lax.dynamic_index_in_dim(routes, my_group, 1, keepdims=False)
    block_ids = jnp.arange(block_count, dtype=jnp.int32)
    block_keys = own_keys.reshape(item_count, block_count, KB, head_dim)
    block_values = own_values.reshape(item_count, block_count, KB, head_dim)
    far_keys, far_values = (
        lax.all_to_all(
            jnp.take(block_keys, requested, axis=1), "blk", split_axis=1, concat_axis=1, tiled=True
        ),
        lax.all_to_all(
            jnp.take(block_values, requested, axis=1),
            "blk",
            split_axis=1,
            concat_axis=1,
            tiled=True,
        ),
    )
    near_keys = jnp.concatenate(
        [own_keys, far_keys.reshape(item_count, cycle_size * KB, head_dim)], axis=1
    )
    near_values = jnp.concatenate(
        [own_values, far_values.reshape(item_count, cycle_size * KB, head_dim)], axis=1
    )
    near_count = near_keys.shape[1]
    item_sub = (my_rank * item_count + jnp.arange(item_count, dtype=jnp.int32)) % sub_count
    far_visible = jnp.repeat(jnp.arange(cycle_size, dtype=jnp.int32) < my_group, KB)
    own_offsets = jnp.arange(group_keys, dtype=jnp.int32) * key_stride
    block_rows = 1024

    def attend(row_block, carried):
        query_out, key_acc, value_acc = carried
        row_start = row_block * block_rows
        queries = lax.dynamic_slice_in_dim(local_query, row_start, block_rows, 1)
        grad_rows = lax.dynamic_slice_in_dim(local_grad, row_start, block_rows, 1)
        row_ids = row_start + jnp.arange(block_rows, dtype=jnp.int32)
        positions = (
            row_ids[None, :] // sub_length * token_count
            + item_sub[:, None] * sub_length
            + row_ids[None, :] % sub_length
        )
        own_visible = own_offsets[None, None, :] <= positions[:, :, None]
        visible = jnp.concatenate(
            [
                own_visible,
                jnp.broadcast_to(far_visible, (item_count, block_rows, far_visible.shape[0])),
            ],
            axis=2,
        )
        scores = (
            jnp.einsum("ird,ikd->irk", queries, near_keys, preferred_element_type=jnp.float32)
            * score_scale
        )
        row_max = jnp.max(jnp.where(visible, scores, -jnp.inf), axis=-1, keepdims=True)
        expsum = jnp.where(visible, jnp.exp(scores - row_max), 0.0)
        weights = expsum / jnp.sum(expsum, axis=-1, keepdims=True)
        weights_half = weights.astype(jnp.bfloat16)
        attended = jnp.einsum(
            "irk,ikd->ird", weights_half, near_values, preferred_element_type=jnp.float32
        )
        delta_rows = jnp.sum(grad_rows.astype(jnp.float32) * attended, axis=-1, keepdims=True)
        dweights = jnp.einsum(
            "ird,ikd->irk", grad_rows, near_values, preferred_element_type=jnp.float32
        )
        dscore = (weights * (dweights - delta_rows)).astype(jnp.bfloat16)
        query_part = (
            jnp.einsum("irk,ikd->ird", dscore, near_keys, preferred_element_type=jnp.float32)
            * score_scale
        ).astype(jnp.bfloat16)
        key_acc = (
            key_acc
            + jnp.einsum("irk,ird->ikd", dscore, queries, preferred_element_type=jnp.float32)
            * score_scale
        )
        value_acc = value_acc + jnp.einsum(
            "irk,ird->ikd", weights_half, grad_rows, preferred_element_type=jnp.float32
        )
        query_out = lax.dynamic_update_slice_in_dim(query_out, query_part, row_start, 1)
        return (query_out, key_acc, value_acc)

    start_state = (
        jnp.zeros((item_count, row_count, head_dim), jnp.bfloat16),
        jnp.zeros((item_count, near_count, head_dim), jnp.float32),
        jnp.zeros((item_count, near_count, head_dim), jnp.float32),
    )
    query_out, key_acc, value_acc = lax.fori_loop(0, row_count // block_rows, attend, start_state)
    own_key_grad = key_acc[:, :group_keys]
    own_value_grad = value_acc[:, :group_keys]
    far_key_grad = key_acc[:, group_keys:].reshape(item_count, cycle_size, KB, head_dim)
    far_value_grad = value_acc[:, group_keys:].reshape(item_count, cycle_size, KB, head_dim)
    back_keys, back_values = (
        lax.all_to_all(far_key_grad, "blk", split_axis=1, concat_axis=1, tiled=True),
        lax.all_to_all(far_value_grad, "blk", split_axis=1, concat_axis=1, tiled=True),
    )
    placer = (requested[:, None] == block_ids[None, :]).astype(jnp.float32)
    added_keys = jnp.einsum(
        "gb,igkd->ibkd", placer, back_keys, precision=lax.Precision.HIGHEST
    ).reshape(item_count, group_keys, head_dim)
    added_values = jnp.einsum(
        "gb,igkd->ibkd", placer, back_values, precision=lax.Precision.HIGHEST
    ).reshape(item_count, group_keys, head_dim)
    key_share = (own_key_grad + added_keys).astype(jnp.bfloat16)
    value_share = (own_value_grad + added_values).astype(jnp.bfloat16)
    query_back, key_back, value_back = (
        lax.all_to_all(query_out, "ulysses", split_axis=1, concat_axis=0, tiled=True),
        lax.all_to_all(key_share, "ulysses", split_axis=1, concat_axis=0, tiled=True),
        lax.all_to_all(value_share, "ulysses", split_axis=1, concat_axis=0, tiled=True),
    )
    query_grad = query_back.reshape(head_count, token_count, head_dim)
    key_grad = jnp.sum(
        key_back.astype(jnp.float32).reshape(head_count, sub_count, -1, head_dim), axis=1
    )
    value_grad = jnp.sum(
        value_back.astype(jnp.float32).reshape(head_count, sub_count, -1, head_dim), axis=1
    )
    return (query_grad, key_grad, value_grad)


def solution(mesh):
    return jax.shard_map(
        body,
        mesh=mesh,
        in_specs=(
            P(None, ("blk", "ulysses"), None),
            P(None, ("blk", "ulysses"), None),
            P(None, "blk", None),
            P(None, "blk", None),
            P(),
        ),
        out_specs=(
            P(None, ("blk", "ulysses"), None),
            P(None, ("blk", "ulysses"), None),
            P(None, ("blk", "ulysses"), None),
        ),
        check_vma=False,
    )
```

profile of v0, /device:TPU:0, one launch (start us, length us, event | category | flops | bytes accessed | tf_op | source)
XLA Modules:
  0.0 155.4 jit_solution(3819428733041253633)
XLA Ops:
  0.6 0.0 copy-start
  0.7 0.7 copy-done
  1.3 0.2 dynamic-slice_reduce_fusion
  1.5 1.0 constant_dynamic-slice_fusion
  2.5 0.0 copy-start.5
  2.5 0.0 copy-start.3
  2.6 0.6 gather_fusion
  3.1 0.6 gather_fusion.1
  3.7 0.1 select_bitcast_fusion
  3.8 8.2 %all_to_all.92 = bf16[4,4,16,128]{3,2,0,1:T(8,128)(2,1)S(1)} all-to-all(bf16[4,4,16,128]{3,2,0,1:T(8,128)(2,1)S(1)} %get-tuple-element.29), channel_id=1, replica_groups=mesh['blk'=4,'ulysses'=8] {'blk'}, dimensions={1} | all-to-all | bytes 131072 | tf_op jit(solution)/shard_map/all_to_all | solution.py:39
  11.9 6.5 %all_to_all.93 = bf16[4,4,16,128]{3,2,0,1:T(8,128)(2,1)S(1)} all-to-all(bf16[4,4,16,128]{3,2,0,1:T(8,128)(2,1)S(1)} %get-tuple-element.28), channel_id=1, replica_groups=mesh['blk'=4,'ulysses'=8] {'blk'}, dimensions={1} | all-to-all | bytes 131072 | tf_op jit(solution)/shard_map/all_to_all | solution.py:42
  18.4 31.4 %all_to_all.94 = bf16[32,128,128]{2,1,0:T(8,128)(2,1)S(1)} all-to-all(bf16[32,128,128]{2,1,0:T(8,128)(2,1)} %param.7), channel_id=1, replica_groups=mesh['blk'=4,'ulysses'=8] {'ulysses'}, dimensions={0} | all-to-all | bytes 2097152 | tf_op jit(solution)/shard_map/all_to_all | solution.py:28
  49.8 3.6 %all-to-all-start.3 = ((bf16[32,128,128]{2,1,0:T(8,128)(2,1)}), bf16[32,128,128]{2,1,0:T(8,128)(2,1)S(1)}, u32[]{:S(2)}, u32[]{:S(2)}) async-start(bf16[32,128,128]{2,1,0:T(8,128)(2,1)} %param.8), calls=%async_computation.3 | async-start | bytes 2097152 | tf_op jit(solution)/shard_map/all_to_all | solution.py:29
  53.4 0.1 broadcast_in_dim.43
  53.5 0.1 reshape.186
  53.6 1.0 broadcast_compare_fusion
  54.6 0.6 copy.32
  55.3 0.1 copy.31
  55.4 23.6 %all-to-all-done.3 = bf16[32,128,128]{2,1,0:T(8,128)(2,1)S(1)} async-done(((bf16[32,128,128]{2,1,0:T(8,128)(2,1)}), bf16[32,128,128]{2,1,0:T(8,128)(2,1)S(1)}, u32[]{:S(2)}, u32[]{:S(2)}) %all-to-all-start.3) | async-done | bytes 1048608 | tf_op jit(solution)/shard_map/all_to_all | solution.py:29
  79.0 1.0 copy.33
  80.0 4.5 %fusion.40 = (f32[4,1024]{1,0:T(4,128)S(1)}, f32[4,1024,192]{1,2,0:T(8,128)}) fusion(pred[4,1024,128]{1,2,0:T(32,128)(4,1)} %broadcast_compare_fusion, pred[192]{0:T(512)(128)(4,1)S(1)} %pad.5.clone, bf16[4,1024,128]{2,1,0:T(8,128)(2,1)S(1)} %bitcast.73, bf16[4,64,128]{2,1,0:T(8,128)(2,1)S(1)} %bitcast.90, bf16[4,128,128]{2,1,0:T(8,128)(2,1)S(1)} %get-tuple-element.33), kind=kOutput, calls=%fused_computation.69 | convolution fusion | flops 409731264 | bytes 4931776 | tf_op jit(solution)/shard_map/while/body/eval_jaxpr/sub | solution.py:86
  84.5 0.0 copy-start.6
  84.6 2.4 %fusion.8 = bf16[4,1024,192]{1,2,0:T(8,128)(2,1)S(1)} fusion(f32[4,1024,192]{1,2,0:T(8,128)} %get-tuple-element.31, f32[4,1024]{1,0:T(4,128)S(1)} %get-tuple-element.30), kind=kLoop, calls=%fused_computation.17 | loop fusion | flops 1572864 | bytes 4734976 | tf_op jit(solution)/shard_map/while/body/eval_jaxpr/convert_element_type | solution.py:88
  87.0 0.6 fusion.41
  87.6 0.7 copy.42
  88.2 3.3 %all-to-all-start.7 = ((f32[4,4,16,128]{3,2,0,1:T(8,128)}), f32[4,4,16,128]{3,2,0,1:T(8,128)S(1)}, u32[]{:S(2)}, u32[]{:S(2)}) async-start(f32[4,4,16,128]{3,2,0,1:T(8,128)} %copy.42), calls=%async_computation.7 | async-start | bytes 262144 | tf_op jit(solution)/shard_map/all_to_all | solution.py:124
  91.6 0.0 copy-start.2
  91.6 2.5 %multiply_reduce_fusion = f32[4,1024]{1,0:T(4,128)S(1)} fusion(bf16[4,1024,128]{2,1,0:T(8,128)(2,1)} %bitcast.75, bf16[4,1024,192]{1,2,0:T(8,128)(2,1)S(1)} %fusion.8, bf16[4,64,128]{2,1,0:T(8,128)(2,1)S(1)} %bitcast.92, bf16[4,128,128]{2,1,0:T(8,128)(2,1)S(1)} %copy-done.6), kind=kOutput, calls=%fused_computation.12 | convolution fusion | flops 203288576 | bytes 2834432 | tf_op jit(solution)/shard_map/while/body/eval_jaxpr/irk,ikd->ird/dot_general | solution.py:89
  94.1 2.5 %fusion.1 = bf16[4,1024,192]{1,2,0:T(8,128)(2,1)S(1)} fusion(bf16[4,1024,128]{2,1,0:T(8,128)(2,1)S(1)} %bitcast.77, f32[4,1024]{1,0:T(4,128)S(1)} %multiply_reduce_fusion, f32[4,1024,192]{1,2,0:T(8,128)} %get-tuple-element.31, f32[4,1024]{1,0:T(4,128)S(1)} %get-tuple-element.30, bf16[4,64,128]{2,1,0:T(8,128)(2,1)S(1)} %bitcast.93, ...), kind=kOutput, calls=%fused_computation.4 | convolution fusion | flops 204865536 | bytes 5996544 | tf_op jit(solution)/shard_map/while/body/eval_jaxpr/ird,ikd->irk/dot_general | solution.py:93
  96.6 0.6 convolution_multiply_fusion
  97.2 0.7 copy.37
  97.9 3.3 %all-to-all-start.5 = ((f32[4,4,16,128]{3,2,0,1:T(8,128)}), f32[4,4,16,128]{3,2,0,1:T(8,128)S(1)}, u32[]{:S(2)}, u32[]{:S(2)}) async-start(f32[4,4,16,128]{3,2,0,1:T(8,128)} %copy.37), calls=%async_computation.5 | async-start | bytes 262144 | tf_op jit(solution)/shard_map/all_to_all | solution.py:123
  101.2 0.4 convolution_bitcast_fusion
  101.7 0.8 copy.45
  102.5 3.3 %all-to-all-done.5 = f32[4,4,16,128]{3,2,0,1:T(8,128)S(1)} async-done(((f32[4,4,16,128]{3,2,0,1:T(8,128)}), f32[4,4,16,128]{3,2,0,1:T(8,128)S(1)}, u32[]{:S(2)}, u32[]{:S(2)}) %all-to-all-start.5) | async-done | bytes 131104 | tf_op jit(solution)/shard_map/all_to_all | solution.py:123
  105.8 3.4 %all-to-all-start.8 = ((bf16[4,128,128]{2,0,1:T(4,128)(2,1)}), bf16[4,128,128]{2,0,1:T(4,128)(2,1)S(1)}, u32[]{:S(2)}, u32[]{:S(2)}) async-start(bf16[4,128,128]{2,0,1:T(4,128)(2,1)} %copy.45), calls=%async_computation.8 | async-start | bytes 262144 | tf_op jit(solution)/shard_map/all_to_all | solution.py:138
  109.2 0.4 convolution_bitcast_fusion.1
  109.7 0.8 copy.40
  110.5 6.1 %all-to-all-done.8 = bf16[4,128,128]{2,0,1:T(4,128)(2,1)S(1)} async-done(((bf16[4,128,128]{2,0,1:T(4,128)(2,1)}), bf16[4,128,128]{2,0,1:T(4,128)(2,1)S(1)}, u32[]{:S(2)}, u32[]{:S(2)}) %all-to-all-start.8) | async-done | bytes 131104 | tf_op jit(solution)/shard_map/all_to_all | solution.py:138
  116.6 3.4 %all-to-all-start.6 = ((bf16[4,128,128]{2,0,1:T(4,128)(2,1)}), bf16[4,128,128]{2,0,1:T(4,128)(2,1)S(1)}, u32[]{:S(2)}, u32[]{:S(2)}) async-start(bf16[4,128,128]{2,0,1:T(4,128)(2,1)} %copy.40), calls=%async_computation.6 | async-start | bytes 262144 | tf_op jit(solution)/shard_map/all_to_all | solution.py:137
  120.0 1.0 multiply_convert_fusion
  120.9 1.8 %copy.35 = bf16[4,1024,128]{2,0,1:T(4,128)(2,1)} copy(bf16[4,1024,128]{2,1,0:T(8,128)(2,1)S(1)} %multiply_convert_fusion) | data formatting | bytes 2097152 | tf_op jit(solution)/shard_map/while/body/eval_jaxpr/convert_element_type | solution.py:100
  122.7 4.5 %all-to-all-done.6 = bf16[4,128,128]{2,0,1:T(4,128)(2,1)S(1)} async-done(((bf16[4,128,128]{2,0,1:T(4,128)(2,1)}), bf16[4,128,128]{2,0,1:T(4,128)(2,1)S(1)}, u32[]{:S(2)}, u32[]{:S(2)}) %all-to-all-start.6) | async-done | bytes 131104 | tf_op jit(solution)/shard_map/all_to_all | solution.py:137
  127.2 3.6 %all-to-all-start.4 = ((bf16[4,1024,128]{2,0,1:T(4,128)(2,1)}), bf16[4,1024,128]{2,0,1:T(4,128)(2,1)S(1)}, u32[]{:S(2)}, u32[]{:S(2)}) async-start(bf16[4,1024,128]{2,0,1:T(4,128)(2,1)} %copy.35), calls=%async_computation.4 | async-start | bytes 2097152 | tf_op jit(solution)/shard_map/all_to_all | solution.py:136
  130.8 0.7 copy.46
  131.6 0.7 copy.41
  132.3 21.9 %all-to-all-done.4 = bf16[4,1024,128]{2,0,1:T(4,128)(2,1)S(1)} async-done(((bf16[4,1024,128]{2,0,1:T(4,128)(2,1)}), bf16[4,1024,128]{2,0,1:T(4,128)(2,1)S(1)}, u32[]{:S(2)}, u32[]{:S(2)}) %all-to-all-start.4) | async-done | bytes 1048608 | tf_op jit(solution)/shard_map/all_to_all | solution.py:136
  154.2 1.2 copy.36
  (31 shorter events, 0.3 us)
Async XLA Ops:
  0.6 0.7 copy-start
  2.5 52.8 %copy-start.5 = (bf16[4,128,128]{2,1,0:T(8,128)(2,1)}, bf16[4,128,128]{2,1,0:T(8,128)(2,1)S(1)}, u32[]{:S(2)}) copy-start(bf16[4,128,128]{2,1,0:T(8,128)(2,1)S(1)} %get-tuple-element.32) | copy-start | bytes 393220
  2.5 77.5 %copy-start.3 = (bf16[4,128,128]{2,1,0:T(8,128)(2,1)}, bf16[4,128,128]{2,1,0:T(8,128)(2,1)S(1)}, u32[]{:S(2)}) copy-start(bf16[4,128,128]{2,1,0:T(8,128)(2,1)S(1)} %get-tuple-element.33) | copy-start | bytes 393220
  49.8 29.2 %all-to-all-start.3 = ((bf16[32,128,128]{2,1,0:T(8,128)(2,1)}), bf16[32,128,128]{2,1,0:T(8,128)(2,1)S(1)}, u32[]{:S(2)}, u32[]{:S(2)}) async-start(bf16[32,128,128]{2,1,0:T(8,128)(2,1)} %param.8), calls=%async_computation.3 | async-start | bytes 2097152 | tf_op jit(solution)/shard_map/all_to_all | solution.py:29
  54.6 29.9 %copy-start.7 = (bf16[4,4,16,128]{3,2,1,0:T(8,128)(2,1)}, bf16[4,4,16,128]{3,2,1,0:T(8,128)(2,1)S(1)}, u32[]{:S(2)}) copy-start(bf16[4,4,16,128]{3,2,1,0:T(8,128)(2,1)S(1)} %copy.30) | copy-start | bytes 196612
  84.5 2.5 %copy-start.1 = (bf16[8,4,128,128]{3,2,0,1:T(8,128)(2,1)S(1)}, bf16[8,4,128,128]{3,2,0,1:T(8,128)(2,1)}, u32[]{:S(2)}) copy-start(bf16[8,4,128,128]{3,2,0,1:T(8,128)(2,1)} %copy.33) | copy-start | bytes 3145732
  84.5 7.1 %copy-start.6 = (bf16[4,128,128]{2,1,0:T(8,128)(2,1)S(1)}, bf16[4,128,128]{2,1,0:T(8,128)(2,1)}, u32[]{:S(2)}) copy-start(bf16[4,128,128]{2,1,0:T(8,128)(2,1)} %copy-done.5) | copy-start | bytes 393220
  84.5 7.1 %copy-start.9 = (bf16[4,4,16,128]{3,2,1,0:T(8,128)(2,1)S(1)}, bf16[4,4,16,128]{3,2,1,0:T(8,128)(2,1)}, u32[]{:S(2)}) copy-start(bf16[4,4,16,128]{3,2,1,0:T(8,128)(2,1)} %copy.32) | copy-start | bytes 196612
  88.2 9.6 %all-to-all-start.7 = ((f32[4,4,16,128]{3,2,0,1:T(8,128)}), f32[4,4,16,128]{3,2,0,1:T(8,128)S(1)}, u32[]{:S(2)}, u32[]{:S(2)}) async-start(f32[4,4,16,128]{3,2,0,1:T(8,128)} %copy.42), calls=%async_computation.7 | async-start | bytes 262144 | tf_op jit(solution)/shard_map/all_to_all | solution.py:124
  91.6 2.5 %copy-start.2 = (bf16[8,4,128,128]{3,2,0,1:T(8,128)(2,1)S(1)}, bf16[8,4,128,128]{3,2,0,1:T(8,128)(2,1)}, u32[]{:S(2)}) copy-start(bf16[8,4,128,128]{3,2,0,1:T(8,128)(2,1)} %copy.33) | copy-start | bytes 3145732
  97.2 22.8 %copy-start.4 = (bf16[4,128,128]{2,1,0:T(8,128)(2,1)S(1)}, bf16[4,128,128]{2,1,0:T(8,128)(2,1)}, u32[]{:S(2)}) copy-start(bf16[4,128,128]{2,1,0:T(8,128)(2,1)} %copy-done.3) | copy-start | bytes 393220
  97.2 22.8 %copy-start.8 = (bf16[4,4,16,128]{3,2,1,0:T(8,128)(2,1)S(1)}, bf16[4,4,16,128]{3,2,1,0:T(8,128)(2,1)}, u32[]{:S(2)}) copy-start(bf16[4,4,16,128]{3,2,1,0:T(8,128)(2,1)} %copy-done.7) | copy-start | bytes 196612
  97.9 7.9 %all-to-all-start.5 = ((f32[4,4,16,128]{3,2,0,1:T(8,128)}), f32[4,4,16,128]{3,2,0,1:T(8,128)S(1)}, u32[]{:S(2)}, u32[]{:S(2)}) async-start(f32[4,4,16,128]{3,2,0,1:T(8,128)} %copy.37), calls=%async_computation.5 | async-start | bytes 262144 | tf_op jit(solution)/shard_map/all_to_all | solution.py:123
  105.8 10.8 %all-to-all-start.8 = ((bf16[4,128,128]{2,0,1:T(4,128)(2,1)}), bf16[4,128,128]{2,0,1:T(4,128)(2,1)S(1)}, u32[]{:S(2)}, u32[]{:S(2)}) async-start(bf16[4,128,128]{2,0,1:T(4,128)(2,1)} %copy.45), calls=%async_computation.8 | async-start | bytes 262144 | tf_op jit(solution)/shard_map/all_to_all | solution.py:138
  116.6 10.7 %all-to-all-start.6 = ((bf16[4,128,128]{2,0,1:T(4,128)(2,1)}), bf16[4,128,128]{2,0,1:T(4,128)(2,1)S(1)}, u32[]{:S(2)}, u32[]{:S(2)}) async-start(bf16[4,128,128]{2,0,1:T(4,128)(2,1)} %copy.40), calls=%async_computation.6 | async-start | bytes 262144 | tf_op jit(solution)/shard_map/all_to_all | solution.py:137
  127.2 26.9 %all-to-all-start.4 = ((bf16[4,1024,128]{2,0,1:T(4,128)(2,1)}), bf16[4,1024,128]{2,0,1:T(4,128)(2,1)S(1)}, u32[]{:S(2)}, u32[]{:S(2)}) async-start(bf16[4,1024,128]{2,0,1:T(4,128)(2,1)} %copy.35), calls=%async_computation.4 | async-start | bytes 2097152 | tf_op jit(solution)/shard_map/all_to_all | solution.py:136
where the time goes:
time: 156 us; the launch traced here: 155 us
  waiting for transfers between devices  59.4 us (38%)
  blocking collectives  46 us (29%)
  starting transfers between devices  20.6 us (13%)
  local copies, waits for them, and re-layouts  12.4 us (8%)
  matrix products  12.4 us (8%)
  other arithmetic  3.66 us (2%)
    all_to_all x1, blocking collectives, body(): lax.all_to_all(packed_query, 'ulysses', split_axis=0, concat_axis=1, tile...  31.4 us
    all_to_all x1, waiting for transfers between devices, body(): lax.all_to_all(packed_grad, 'ulysses', split_axis=0, concat_axis=1, tiled...  23.6 us
    all_to_all x1, waiting for transfers between devices, body(): lax.all_to_all(query_out, 'ulysses', split_axis=1, concat_axis=0, tiled=T...  21.9 us
    all_to_all x1, blocking collectives, body(): lax.all_to_all(jnp.take(block_keys, requested, axis=1), 'blk', split_axis...  8.16 us
    all_to_all x1, blocking collectives, body(): lax.all_to_all(jnp.take(block_values, requested, axis=1), 'blk', split_ax...  6.47 us
    all_to_all x1, waiting for transfers between devices, body(): lax.all_to_all(value_share, 'ulysses', split_axis=1, concat_axis=0, tiled...  6.08 us
    all_to_all x1, waiting for transfers between devices, body(): lax.all_to_all(key_share, 'ulysses', split_axis=1, concat_axis=0, tiled=T...  4.52 us
    sub x1, matrix products, attend(): expsum = jnp.where(visible, jnp.exp(scores - row_max), 0.0)  4.49 us
  transfers between devices with their start and end apart: 6, of which 5 were waited for; matrix products, arithmetic and copies ran while one was open for 10% of the time, Pallas kernels for 0%

commit v1 on v0

v1 whole, which is shorter than its diff:
```python
import functools
import math

import jax
import jax.numpy as jnp
from jax import lax
from jax.experimental import pallas as pl
from jax.experimental.pallas import tpu as pltpu
from jax.sharding import PartitionSpec as P

KB = 16
CHUNKS = 1


def attend_kernel(far_slots, place, query, grad, keys, values, *rest):
    far_rows = rest[:far_slots]
    query_out, own_out = rest[-2 - far_slots :][:2]
    far_outs = rest[len(rest) - far_slots :]
    heads, tokens, head_dim = query.shape
    group_keys = keys.shape[1]
    group, first_token, key_stride = place[0], place[1], place[2]
    score_scale = 1.0 / math.sqrt(head_dim)
    exp_scale = score_scale * math.log2(math.e)
    key_at = lax.broadcasted_iota(jnp.int32, (group_keys, tokens), 0) * key_stride
    token_at = lax.broadcasted_iota(jnp.int32, (group_keys, tokens), 1) + first_token
    own_hidden = jnp.where(key_at <= token_at, 0.0, -jnp.inf)
    hidden = [own_hidden]
    for slot in range(far_slots):
        seen = jnp.where(group >= slot + 1, 0.0, -jnp.inf)
        hidden.append(jnp.full((KB, tokens), seen, jnp.float32))
    hidden = jnp.concatenate(hidden, axis=0)
    nt = (((1,), (1,)), ((), ()))
    tn = (((0,), (0,)), ((), ()))
    for head in range(heads):
        q = query[head]
        g = grad[head]
        near_keys = jnp.concatenate([keys[head]] + [f[0, head] for f in far_rows], axis=0)
        near_values = jnp.concatenate([values[head]] + [f[1, head] for f in far_rows], axis=0)
        scores = lax.dot_general(near_keys, q, nt, preferred_element_type=jnp.float32) + hidden
        dweights = lax.dot_general(near_values, g, nt, preferred_element_type=jnp.float32)
        row_max = jnp.max(scores, axis=0, keepdims=True)
        expsum = jnp.exp2((scores - row_max) * exp_scale)
        weights = expsum * (1.0 / jnp.sum(expsum, axis=0, keepdims=True))
        weights_half = weights.astype(jnp.bfloat16)
        delta = jnp.sum(weights_half.astype(jnp.float32) * dweights, axis=0, keepdims=True)
        dscore = (weights * (dweights - delta)).astype(jnp.bfloat16)
        query_grad = lax.dot_general(dscore, near_keys, tn, preferred_element_type=jnp.float32)
        query_out[head] = (query_grad * score_scale).astype(jnp.bfloat16)
        key_part = jnp.dot(dscore, q, preferred_element_type=jnp.float32) * score_scale
        value_part = jnp.dot(weights_half, g, preferred_element_type=jnp.float32)
        key_part = key_part.astype(jnp.bfloat16)
        value_part = value_part.astype(jnp.bfloat16)
        own_out[0, head] = key_part[:group_keys]
        own_out[1, head] = value_part[:group_keys]
        for slot, far_out in enumerate(far_outs):
            rows = slice(group_keys + slot * KB, group_keys + (slot + 1) * KB)
            far_out[0, head] = key_part[rows]
            far_out[1, head] = value_part[rows]


def attend(place, query, grad, keys, values, far, first_head, chunk_heads, query_out):
    head_count, tokens, head_dim = query.shape
    group_keys = keys.shape[1]
    step_heads = math.gcd(4, chunk_heads)
    first_step = first_head // step_heads

    def rows(count):
        return pl.BlockSpec((step_heads, count, head_dim), lambda i, place: (i + first_step, 0, 0))

    def pair(count):
        return pl.BlockSpec((2, step_heads, count, head_dim), lambda i, place: (0, i, 0, 0))

    operands = [place, query, grad, keys, values, *far]
    in_specs = [rows(tokens), rows(tokens), rows(group_keys), rows(group_keys)]
    in_specs += [pair(KB)] * len(far)
    aliases = {}
    if query_out is not None:
        aliases = {len(operands): 0}
        operands.append(query_out)
        in_specs.append(pl.BlockSpec(memory_space=pl.ANY))
    outs = pl.pallas_call(
        functools.partial(attend_kernel, len(far)),
        out_shape=[
            jax.ShapeDtypeStruct(query.shape, jnp.bfloat16),
            jax.ShapeDtypeStruct((2, chunk_heads, group_keys, head_dim), jnp.bfloat16),
        ]
        + [jax.ShapeDtypeStruct((2, chunk_heads, KB, head_dim), jnp.bfloat16)] * len(far),
        grid_spec=pltpu.PrefetchScalarGridSpec(
            num_scalar_prefetch=1,
            grid=(chunk_heads // step_heads,),
            in_specs=in_specs,
            out_specs=[rows(tokens), pair(group_keys)] + [pair(KB)] * len(far),
        ),
        input_output_aliases=aliases,
        name="attend",
    )(*operands)
    return outs[0], outs[1], outs[2:]


def swap_pairs(size, bit):
    return [(rank, rank ^ bit) for rank in range(size)]


def body(query_rows, out_grad, key_rows, value_rows, routes):
    head_count, token_count, head_dim = query_rows.shape
    group_keys = key_rows.shape[1]
    groups = lax.axis_size("blk")
    ranks = lax.axis_size("ulysses")
    my_group = lax.axis_index("blk")
    my_rank = lax.axis_index("ulysses")
    block_count = group_keys // KB
    key_stride = token_count * ranks // group_keys
    rank_keys = group_keys // ranks
    place = jnp.stack([my_group, my_rank * token_count, jnp.int32(key_stride)]).astype(jnp.int32)
    chunk_heads = head_count // CHUNKS
    bits = [1 << b for b in range(ranks.bit_length() - 1)]
    orders = [bits]

    def route(asker, holder):
        return routes[jnp.clip(asker, 0, groups - 1), jnp.clip(holder, 0, groups - 1)]

    key_blocks = key_rows.reshape(head_count, block_count, KB, head_dim)
    value_blocks = value_rows.reshape(head_count, block_count, KB, head_dim)

    def routed(first_head, distance):
        block = route(my_group + distance, my_group)
        picked = [
            lax.dynamic_slice(
                rows, (first_head, block, 0, 0), (chunk_heads, 1, KB, head_dim)
            ).reshape(chunk_heads, KB, head_dim)
            for rows in (key_blocks, value_blocks)
        ]
        pairs = [(g, g + distance) for g in range(groups - distance)]
        return lax.ppermute(jnp.stack(picked), "blk", pairs)

    def send_back(part, distance):
        pairs = [(g + distance, g) for g in range(groups - distance)]
        return lax.ppermute(part, "blk", pairs)

    def add_back(own, back):
        total = own.reshape(2, chunk_heads, block_count, KB, head_dim).astype(jnp.float32)
        block_ids = jnp.arange(block_count, dtype=jnp.int32)[None, None, :, None, None]
        for distance, part in enumerate(back, 1):
            block = route(my_group + distance, my_group)
            total = total + jnp.where(
                block_ids == block, part[:, :, None].astype(jnp.float32), 0.0
            )
        return total.astype(jnp.bfloat16)

    def scatter(total, order):
        shape = (2, chunk_heads) + (2,) * len(bits) + (rank_keys, head_dim)
        total = total.reshape(shape)
        left = list(reversed(bits))
        for bit in order:
            axis = 2 + left.index(bit)
            mine = (my_rank // bit) % 2
            sent = lax.dynamic_index_in_dim(total, 1 - mine, axis, keepdims=False)
            kept = lax.dynamic_index_in_dim(total, mine, axis, keepdims=False)
            came = lax.ppermute(sent, "ulysses", swap_pairs(ranks, bit))
            left.remove(bit)
            total = kept.astype(jnp.float32) + came.astype(jnp.float32)
            if left:
                total = total.astype(jnp.bfloat16)
        return total

    far = [
        [routed(chunk * chunk_heads, d) for d in range(1, groups)] for chunk in range(CHUNKS)
    ]
    query_out = None
    results = []
    for chunk in range(CHUNKS):
        query_out, own, parts = attend(
            place, query_rows, out_grad, key_rows, value_rows, far[chunk],
            chunk * chunk_heads, chunk_heads, query_out,
        )
        back = [send_back(part, d) for d, part in enumerate(parts, 1)]
        results.append(scatter(add_back(own, back), orders[chunk % len(orders)]))
    key_grad = jnp.concatenate([r[0] for r in results], axis=0)
    value_grad = jnp.concatenate([r[1] for r in results], axis=0)
    return (query_out, key_grad, value_grad)


def solution(mesh):
    return jax.shard_map(
        body,
        mesh=mesh,
        in_specs=(
            P(None, ("blk", "ulysses"), None),
            P(None, ("blk", "ulysses"), None),
            P(None, "blk", None),
            P(None, "blk", None),
            P(),
        ),
        out_specs=(
            P(None, ("blk", "ulysses"), None),
            P(None, ("blk", "ulysses"), None),
            P(None, ("blk", "ulysses"), None),
        ),
        check_vma=False,
    )
```

time: 156 us -> 111 us (0.71)
  blocking collectives: 46 us -> 0 us
  Pallas kernels: 0 us -> 14.7 us
  matrix products: 12.4 us -> 0 us
  local copies, waits for them, and re-layouts: 12.4 us -> 4.64 us
  between operations: 0.94 us -> 6.49 us
  starting transfers between devices: 20.6 us -> 17.9 us
  other arithmetic: 3.66 us -> 5.9 us
  waiting for transfers between devices: 59.4 us -> 61 us
    ppermute x0 -> x9, waiting for transfers between devices: none -> 61 us  [the longest x3 46.8 us: scatter(): came = lax.ppermute(sent, 'ulysses', swap_pairs(ranks, bit))]
    all_to_all x6 -> x0, waiting for transfers between devices: 59.4 us -> none  [the longest x1 23.6 us: body(): lax.all_to_all(packed_grad, 'ulysses', split_axis=0, concat_axis=1, tiled...]
    all_to_all x3 -> x0, blocking collectives: 46 us -> none  [the longest x1 31.4 us: body(): lax.all_to_all(packed_query, 'ulysses', split_axis=0, concat_axis=1, tile...]
    all_to_all x6 -> x0, starting transfers between devices: 20.6 us -> none  [the longest x1 3.59 us: body(): lax.all_to_all(packed_grad, 'ulysses', split_axis=0, concat_axis=1, tiled...]
    ppermute x0 -> x9, starting transfers between devices: none -> 17.9 us  [the longest x3 8.15 us: routed(): return lax.ppermute(jnp.stack(picked), 'blk', pairs)]
    pallas_call x0 -> x1, Pallas kernels: none -> 14.7 us  [attend(): pl.pallas_call(functools.partial(attend_kernel, len(far)), out_shape=[jax...]
    dot_general x7 -> x0, matrix products: 7.88 us -> none  [the longest x1 2.5 us: attend(): jnp.einsum('ird,ikd->irk', grad_rows, near_values, preferred_element_type...]
    convert_element_type x5 -> x0, local copies, waits for them, and re-layouts: 4.75 us -> none  [the longest x1 1.78 us: attend(): query_part = (jnp.einsum('irk,ikd->ird', dscore, near_keys, preferred_ele...]
  transfers between devices with their start and end apart: 6 -> 9, of which waited for: 5 -> 7; matrix products, arithmetic and copies ran while one was open for 10% -> 3% of each run, Pallas kernels for 0% -> 0%
where the time goes in v1:
time: 111 us
  waiting for transfers between devices  61 us (55%)
  starting transfers between devices  17.9 us (16%)
  Pallas kernels  14.7 us (13%)
  between operations  6.49 us (6%)
  other arithmetic  5.9 us (5%)
  local copies, waits for them, and re-layouts  4.64 us (4%)
    ppermute x3, waiting for transfers between devices, scatter(): came = lax.ppermute(sent, 'ulysses', swap_pairs(ranks, bit))  46.8 us
    pallas_call x1, Pallas kernels, attend(): pl.pallas_call(functools.partial(attend_kernel, len(far)), out_shape=[jax...  14.7 us
    ppermute x3, starting transfers between devices, routed(): return lax.ppermute(jnp.stack(picked), 'blk', pairs)  8.15 us
    ppermute x3, waiting for transfers between devices, routed(): return lax.ppermute(jnp.stack(picked), 'blk', pairs)  7.72 us
    ppermute x3, waiting for transfers between devices, send_back(): return lax.ppermute(part, 'blk', pairs)  6.56 us
    ppermute x3, starting transfers between devices, scatter(): came = lax.ppermute(sent, 'ulysses', swap_pairs(ranks, bit))  5.88 us
    ppermute x3, starting transfers between devices, send_back(): return lax.ppermute(part, 'blk', pairs)  3.87 us
  transfers between devices with their start and end apart: 9, of which 7 were waited for; matrix products, arithmetic and copies ran while one was open for 3% of the time, Pallas kernels for 0%

profile of v1, /device:TPU:0, one launch (start us, length us, event | category | flops | bytes accessed | tf_op | source)
XLA Modules:
  0.0 110.7 jit_solution(2637563946892160047)
XLA Ops:
  0.6 1.5 %fusion.5 = (s32[1,1]{1,0:T(1,128)}, s32[1,1]{1,0:T(1,128)}, s32[1,1]{1,0:T(1,128)}) fusion(s32[4,4]{1,0:T(4,128)} %param.9, s32[]{:T(128)S(6)} %min.24, s32[]{:T(128)S(6)} %min.22, s32[]{:T(128)S(6)} %min.21, s32[]{:T(128)S(6)} %min.23), kind=kLoop, calls=%fused_computation.28 | loop fusion | bytes 40 | tf_op jit(solution)/shard_map/dynamic_slice | solution.py:120
  7.8 1.4 %dynamic-slice_bitcast_fusion.3 = (bf16[1,32,16,128]{3,2,1,0:T(8,128)(2,1)S(1)}, bf16[1,32,16,128]{3,2,1,0:T(8,128)(2,1)S(1)}, bf16[1,32,16,128]{3,2,1,0:T(8,128...) fusion(bf16[32,8,16,128]{3,2,1,0:T(8,128)(2,1)} %bitcast.54, ...), kind=kLoop, calls=%fused_computation.17 | loop fusion | bytes 1572876 | tf_op jit(solution)/shard_map/stack;reshape | solution.py:134
  9.2 2.4 %collective-permute-start = (bf16[2,32,16,128]{3,2,1,0:T(8,128)(2,1)S(1)}, bf16[2,32,16,128]{3,2,1,0:T(8,128)(2,1)S(1)}, u32[]{:S(2)}, u32[]{:S(2)}) collective-permute-start(bf16[2,32,16,128]{3,2,1,0:T(8,128)(2,1)S(1)} %pad_maximum_fusion), channel_id=1, source_target_pairs={{0,8},{8,16},{16,24},{1,9},{9,17},{17,25},{2,10},{10,18},{18,26},{... | collective-permute-start | bytes 786440 | tf_op jit(solution)/shard_map/ppermute | solution.py:134
  11.7 4.4 %collective-permute-start.1 = (bf16[2,32,16,128]{3,2,1,0:T(8,128)(2,1)S(1)}, bf16[2,32,16,128]{3,2,1,0:T(8,128)(2,1)S(1)}, u32[]{:S(2)}, u32[]{:S(2)}) collective-permute-start(bf16[2,32,16,128]{3,2,1,0:T(8,128)(2,1)S(1)} %pad_maximum_fusion.1), channel_id=1, source_target_pairs={{0,16},{8,24},{1,17},{9,25},{2,18},{10,26},{3,19},{11,27},{4,20},{... | collective-permute-start | bytes 786440 | tf_op jit(solution)/shard_map/ppermute | solution.py:134
  16.1 1.3 %collective-permute-start.2 = (bf16[2,32,16,128]{3,2,1,0:T(8,128)(2,1)S(1)}, bf16[2,32,16,128]{3,2,1,0:T(8,128)(2,1)S(1)}, u32[]{:S(2)}, u32[]{:S(2)}) collective-permute-start(bf16[2,32,16,128]{3,2,1,0:T(8,128)(2,1)S(1)} %pad_maximum_fusion.2), channel_id=1, source_target_pairs={{0,24},{1,25},{2,26},{3,27},{4,28},{5,29},{6,30},{7,31}} | collective-permute-start | bytes 786440 | tf_op jit(solution)/shard_map/ppermute | solution.py:134
  17.4 0.7 pad_add_fusion.place
  18.1 0.0 collective-permute-done.rest_0_
  18.1 0.0 copy-start.1
  18.1 4.6 %collective-permute-done.1.rest_1_ = bf16[2,32,16,128]{3,2,1,0:T(8,128)(2,1)S(1)} collective-permute-done((bf16[2,32,16,128]{3,2,1,0:T(8,128)(2,1)S(1)}, bf16[2,32,16,128]{3,2,1,0:T(8,128)(2,1)S(1)}, u32[]{:S(2)}, u32[]{:S(2)}) %collective-permute-start.1) | collective-permute-done | bytes 262176 | tf_op jit(solution)/shard_map/ppermute | solution.py:134
  22.7 0.0 copy-start.2
  22.7 3.1 %collective-permute-done.2.rest_2_ = bf16[2,32,16,128]{3,2,1,0:T(8,128)(2,1)S(1)} collective-permute-done((bf16[2,32,16,128]{3,2,1,0:T(8,128)(2,1)S(1)}, bf16[2,32,16,128]{3,2,1,0:T(8,128)(2,1)S(1)}, u32[]{:S(2)}, u32[]{:S(2)}) %collective-permute-start.2) | collective-permute-done | bytes 262176 | tf_op jit(solution)/shard_map/ppermute | solution.py:134
  25.8 0.0 copy-done.1
  25.8 0.0 copy-done.2
  25.8 0.0 copy-start.3
  25.8 0.7 copy-done.3
  26.5 14.7 %attend.1 = (bf16[32,128,128]{2,1,0:T(8,128)(2,1)}, bf16[2,32,128,128]{3,2,1,0:T(8,128)(2,1)}, bf16[2,32,16,128]{3,2,1,0:T(8,128)(2,1)}, bf16[2,32,16,128]{3,2,1,0:T(8,128)(2,1)}, bf16[2,32,16,128]{3,2,1,0:T(8,128)(2,1)}) custom-call(s32[3]{0:T(128)} %pad_add_fusion.place, bf16[32,128,128]{2,1,0:T(8,128)(2,1)} %query.1, bf16[32,128,128]{2,1,0:T(8,128)(2,1)} %grad.1, ...), custom_call_target="tpu_custom_call" | custom-call | tf_op jit(solution)/shard_map/attend/pallas_call | solution.py:81
  41.3 1.3 %collective-permute-start.5 = (bf16[2,32,16,128]{3,2,1,0:T(8,128)(2,1)}, bf16[2,32,16,128]{3,2,1,0:T(8,128)(2,1)S(1)}, u32[]{:S(2)}, u32[]{:S(2)}) collective-permute-start(bf16[2,32,16,128]{3,2,1,0:T(8,128)(2,1)} %get-tuple-element.12), channel_id=1, source_target_pairs={{24,0},{25,1},{26,2},{27,3},{28,4},{29,5},{30,6},{31,7}} | collective-permute-start | bytes 786440 | tf_op jit(solution)/shard_map/ppermute | solution.py:138
  42.5 1.3 %collective-permute-start.4 = (bf16[2,32,16,128]{3,2,1,0:T(8,128)(2,1)}, bf16[2,32,16,128]{3,2,1,0:T(8,128)(2,1)S(1)}, u32[]{:S(2)}, u32[]{:S(2)}) collective-permute-start(bf16[2,32,16,128]{3,2,1,0:T(8,128)(2,1)} %get-tuple-element.11), channel_id=1, source_target_pairs={{16,0},{24,8},{17,1},{25,9},{18,2},{26,10},{19,3},{27,11},{20,4},{... | collective-permute-start | bytes 786440 | tf_op jit(solution)/shard_map/ppermute | solution.py:138
  43.8 1.3 %collective-permute-start.3 = (bf16[2,32,16,128]{3,2,1,0:T(8,128)(2,1)}, bf16[2,32,16,128]{3,2,1,0:T(8,128)(2,1)S(1)}, u32[]{:S(2)}, u32[]{:S(2)}) collective-permute-start(bf16[2,32,16,128]{3,2,1,0:T(8,128)(2,1)} %get-tuple-element.10), channel_id=1, source_target_pairs={{8,0},{16,8},{24,16},{9,1},{17,9},{25,17},{10,2},{18,10},{26,18},{... | collective-permute-start | bytes 786440 | tf_op jit(solution)/shard_map/ppermute | solution.py:138
  45.2 0.0 copy-start
  45.2 0.8 broadcast_compare_fusion.2
  46.0 1.3 %broadcast_compare_fusion = (pred[2,2,2]{0,1,2:T(4,128)(4,1)S(1)}, pred[2,2,2]{0,1,2:T(4,128)(4,1)S(1)}) fusion(s32[]{:T(128)} %bitcast.10, s32[]{:T(128)} %bitcast.7), kind=kLoop, calls=%fused_computation.24 | loop fusion | flops 48 | bytes 24 | tf_op jit(solution)/shard_map/eq | solution.py:146
  47.2 2.8 %collective-permute-done.5 = bf16[2,32,16,128]{3,2,1,0:T(8,128)(2,1)S(1)} collective-permute-done((bf16[2,32,16,128]{3,2,1,0:T(8,128)(2,1)}, bf16[2,32,16,128]{3,2,1,0:T(8,128)(2,1)S(1)}, u32[]{:S(2)}, u32[]{:S(2)}) %collective-permute-start.5) | collective-permute-done | bytes 262176 | tf_op jit(solution)/shard_map/ppermute | solution.py:138
  50.1 3.7 %collective-permute-done.4 = bf16[2,32,16,128]{3,2,1,0:T(8,128)(2,1)S(1)} collective-permute-done((bf16[2,32,16,128]{3,2,1,0:T(8,128)(2,1)}, bf16[2,32,16,128]{3,2,1,0:T(8,128)(2,1)S(1)}, u32[]{:S(2)}, u32[]{:S(2)}) %collective-permute-start.4) | collective-permute-done | bytes 262176 | tf_op jit(solution)/shard_map/ppermute | solution.py:138
  53.9 0.0 collective-permute-done.3
  53.9 0.0 copy-done
  53.9 1.3 %fusion.2 = bf16[2,32,2,2,2,16,128]{6,5,1,0,2,3,4:T(8,128)(2,1)S(1)} fusion(f32[2,32,16,128]{3,2,1,0:T(8,128)S(1)} %convert_element_type.60, f32[2,32,16,128]{3,2,1,0:T(8,128)S(1)} %convert_element_type.59, f32[2,32,16,128]{3,2,1,0:T(8,128)S(1)} %convert_element_type.58, pred[2,2,2]{0,1,2:T(4,128)(4,1)S(1)} %get-tuple-element.27, ...), kind=kLoop, calls=%fused_computation.3 | loop fusion | flops 8388608 | bytes 5767192 | tf_op jit(solution)/shard_map/convert_element_type | solution.py:148
  55.2 0.2 dynamic-slice_bitcast_fusion
  55.4 1.6 %collective-permute-start.6 = (bf16[2,32,2,2,16,128]{5,4,1,0,2,3:T(8,128)(2,1)S(1)}, bf16[2,32,2,2,16,128]{5,4,1,0,2,3:T(8,128)(2,1)}, u32[]{:S(2)}, u32[]{:S(2)}) collective-permute-start(bf16[2,32,2,2,16,128]{5,4,1,0,2,3:T(8,128)(2,1)S(1)} %dynamic-slice_bitcast_fusion), channel_id=1, source_target_pairs={{0,1},{1,0},{2,3},{3,2},{4,5},{5,4},{6,7},{7,6},{8,9},{9,8},{10,11... | collective-permute-start | bytes 3145736 | tf_op jit(solution)/shard_map/ppermute | solution.py:159
  57.0 22.1 %collective-permute-done.6 = bf16[2,32,2,2,16,128]{5,4,1,0,2,3:T(8,128)(2,1)} collective-permute-done((bf16[2,32,2,2,16,128]{5,4,1,0,2,3:T(8,128)(2,1)S(1)}, bf16[2,32,2,2,16,128]{5,4,1,0,2,3:T(8,128)(2,1)}, u32[]{:S(2)}, u32[]{:S(2)}) %collective-permute-start.6) | collective-permute-done | bytes 1048608 | tf_op jit(solution)/shard_map/ppermute | solution.py:159
  79.1 1.5 %fusion.3 = bf16[2,32,2,2,16,128]{5,4,1,0,2,3:T(8,128)(2,1)S(1)} fusion(bf16[2,32,2,2,16,128]{5,4,1,0,2,3:T(8,128)(2,1)} %collective-permute-done.6, bf16[2,32,2,2,2,16,128]{6,5,1,0,2,3,4:T(8,128)(2,1)S(1)} %fusion.2, s32[]{:T(128)S(6)} %select_n.88), kind=kLoop, calls=%fused_computation.5 | loop fusion | flops 2097152 | bytes 3145732 | tf_op jit(solution)/shard_map/convert_element_type | solution.py:163
  80.6 1.6 %collective-permute-start.7 = (bf16[2,32,2,16,128]{4,3,1,0,2:T(8,128)(2,1)S(1)}, bf16[2,32,2,16,128]{4,3,1,0,2:T(8,128)(2,1)S(1)}, u32[]{:S(2)}, u32[]{:S(2)}) collective-permute-start(bf16[2,32,2,16,128]{4,3,1,0,2:T(8,128)(2,1)S(1)} %dynamic-slice_bitcast_fusion.1), channel_id=1, source_target_pairs={{0,2},{1,3},{2,0},{3,1},{4,6},{5,7},{6,4},{7,5},{8,10},{9,11},{10,... | collective-permute-start | bytes 1572872 | tf_op jit(solution)/shard_map/ppermute | solution.py:159
  82.3 11.8 %collective-permute-done.7 = bf16[2,32,2,16,128]{4,3,1,0,2:T(8,128)(2,1)S(1)} collective-permute-done((bf16[2,32,2,16,128]{4,3,1,0,2:T(8,128)(2,1)S(1)}, bf16[2,32,2,16,128]{4,3,1,0,2:T(8,128)(2,1)S(1)}, u32[]{:S(2)}, u32[]{:S(2)}) %collective-permute-start.7) | collective-permute-done | bytes 524320 | tf_op jit(solution)/shard_map/ppermute | solution.py:159
  94.1 0.1 fusion.4
  94.3 2.7 %collective-permute-start.8 = (bf16[2,32,16,128]{3,2,1,0:T(8,128)(2,1)S(1)}, bf16[2,32,16,128]{3,2,1,0:T(8,128)(2,1)S(1)}, u32[]{:S(2)}, u32[]{:S(2)}) collective-permute-start(bf16[2,32,16,128]{3,2,1,0:T(8,128)(2,1)S(1)} %dynamic-slice_bitcast_fusion.2), channel_id=1, source_target_pairs={{0,4},{1,5},{2,6},{3,7},{4,0},{5,1},{6,2},{7,3},{8,12},{9,13},{10,... | collective-permute-start | bytes 786440 | tf_op jit(solution)/shard_map/ppermute | solution.py:159
  96.9 12.9 %collective-permute-done.8 = bf16[2,32,16,128]{3,2,1,0:T(8,128)(2,1)S(1)} collective-permute-done((bf16[2,32,16,128]{3,2,1,0:T(8,128)(2,1)S(1)}, bf16[2,32,16,128]{3,2,1,0:T(8,128)(2,1)S(1)}, u32[]{:S(2)}, u32[]{:S(2)}) %collective-permute-start.8) | collective-permute-done | bytes 262176 | tf_op jit(solution)/shard_map/ppermute | solution.py:159
  109.8 0.1 convert_add_fusion.2
  109.9 0.8 slice_bitcast_fusion
  (8 shorter events, 0.3 us)
Async XLA Ops:
  9.2 8.9 %collective-permute-start = (bf16[2,32,16,128]{3,2,1,0:T(8,128)(2,1)S(1)}, bf16[2,32,16,128]{3,2,1,0:T(8,128)(2,1)S(1)}, u32[]{:S(2)}, u32[]{:S(2)}) collective-permute-start(bf16[2,32,16,128]{3,2,1,0:T(8,128)(2,1)S(1)} %pad_maximum_fusion), channel_id=1, source_target_pairs={{0,8},{8,16},{16,24},{1,9},{9,17},{17,25},{2,10},{10,18},{18,26},{... | collective-permute-start | bytes 786440 | tf_op jit(solution)/shard_map/ppermute | solution.py:134
  11.7 11.1 %collective-permute-start.1 = (bf16[2,32,16,128]{3,2,1,0:T(8,128)(2,1)S(1)}, bf16[2,32,16,128]{3,2,1,0:T(8,128)(2,1)S(1)}, u32[]{:S(2)}, u32[]{:S(2)}) collective-permute-start(bf16[2,32,16,128]{3,2,1,0:T(8,128)(2,1)S(1)} %pad_maximum_fusion.1), channel_id=1, source_target_pairs={{0,16},{8,24},{1,17},{9,25},{2,18},{10,26},{3,19},{11,27},{4,20},{... | collective-permute-start | bytes 786440 | tf_op jit(solution)/shard_map/ppermute | solution.py:134
  16.1 9.7 %collective-permute-start.2 = (bf16[2,32,16,128]{3,2,1,0:T(8,128)(2,1)S(1)}, bf16[2,32,16,128]{3,2,1,0:T(8,128)(2,1)S(1)}, u32[]{:S(2)}, u32[]{:S(2)}) collective-permute-start(bf16[2,32,16,128]{3,2,1,0:T(8,128)(2,1)S(1)} %pad_maximum_fusion.2), channel_id=1, source_target_pairs={{0,24},{1,25},{2,26},{3,27},{4,28},{5,29},{6,30},{7,31}} | collective-permute-start | bytes 786440 | tf_op jit(solution)/shard_map/ppermute | solution.py:134
  18.1 7.7 %copy-start.1 = (bf16[2,32,16,128]{3,2,1,0:T(8,128)(2,1)}, bf16[2,32,16,128]{3,2,1,0:T(8,128)(2,1)S(1)}, u32[]{:S(2)}) copy-start(bf16[2,32,16,128]{3,2,1,0:T(8,128)(2,1)S(1)} %collective-permute-done.rest_0_) | copy-start | bytes 786436
  22.7 3.1 %copy-start.2 = (bf16[2,32,16,128]{3,2,1,0:T(8,128)(2,1)}, bf16[2,32,16,128]{3,2,1,0:T(8,128)(2,1)S(1)}, u32[]{:S(2)}) copy-start(bf16[2,32,16,128]{3,2,1,0:T(8,128)(2,1)S(1)} %collective-permute-done.1.rest_1_) | copy-start | bytes 786436
  25.8 0.7 copy-start.3
  41.3 8.8 %collective-permute-start.5 = (bf16[2,32,16,128]{3,2,1,0:T(8,128)(2,1)}, bf16[2,32,16,128]{3,2,1,0:T(8,128)(2,1)S(1)}, u32[]{:S(2)}, u32[]{:S(2)}) collective-permute-start(bf16[2,32,16,128]{3,2,1,0:T(8,128)(2,1)} %get-tuple-element.12), channel_id=1, source_target_pairs={{24,0},{25,1},{26,2},{27,3},{28,4},{29,5},{30,6},{31,7}} | collective-permute-start | bytes 786440 | tf_op jit(solution)/shard_map/ppermute | solution.py:138
  42.5 11.3 %collective-permute-start.4 = (bf16[2,32,16,128]{3,2,1,0:T(8,128)(2,1)}, bf16[2,32,16,128]{3,2,1,0:T(8,128)(2,1)S(1)}, u32[]{:S(2)}, u32[]{:S(2)}) collective-permute-start(bf16[2,32,16,128]{3,2,1,0:T(8,128)(2,1)} %get-tuple-element.11), channel_id=1, source_target_pairs={{16,0},{24,8},{17,1},{25,9},{18,2},{26,10},{19,3},{27,11},{20,4},{... | collective-permute-start | bytes 786440 | tf_op jit(solution)/shard_map/ppermute | solution.py:138
  43.8 10.0 %collective-permute-start.3 = (bf16[2,32,16,128]{3,2,1,0:T(8,128)(2,1)}, bf16[2,32,16,128]{3,2,1,0:T(8,128)(2,1)S(1)}, u32[]{:S(2)}, u32[]{:S(2)}) collective-permute-start(bf16[2,32,16,128]{3,2,1,0:T(8,128)(2,1)} %get-tuple-element.10), channel_id=1, source_target_pairs={{8,0},{16,8},{24,16},{9,1},{17,9},{25,17},{10,2},{18,10},{26,18},{... | collective-permute-start | bytes 786440 | tf_op jit(solution)/shard_map/ppermute | solution.py:138
  45.2 8.8 %copy-start = (bf16[2,32,128,128]{3,2,1,0:T(8,128)(2,1)S(1)}, bf16[2,32,128,128]{3,2,1,0:T(8,128)(2,1)}, u32[]{:S(2)}) copy-start(bf16[2,32,128,128]{3,2,1,0:T(8,128)(2,1)} %get-tuple-element.9) | copy-start | bytes 6291460
  55.4 23.7 %collective-permute-start.6 = (bf16[2,32,2,2,16,128]{5,4,1,0,2,3:T(8,128)(2,1)S(1)}, bf16[2,32,2,2,16,128]{5,4,1,0,2,3:T(8,128)(2,1)}, u32[]{:S(2)}, u32[]{:S(2)}) collective-permute-start(bf16[2,32,2,2,16,128]{5,4,1,0,2,3:T(8,128)(2,1)S(1)} %dynamic-slice_bitcast_fusion), channel_id=1, source_target_pairs={{0,1},{1,0},{2,3},{3,2},{4,5},{5,4},{6,7},{7,6},{8,9},{9,8},{10,11... | collective-permute-start | bytes 3145736 | tf_op jit(solution)/shard_map/ppermute | solution.py:159
  80.6 13.5 %collective-permute-start.7 = (bf16[2,32,2,16,128]{4,3,1,0,2:T(8,128)(2,1)S(1)}, bf16[2,32,2,16,128]{4,3,1,0,2:T(8,128)(2,1)S(1)}, u32[]{:S(2)}, u32[]{:S(2)}) collective-permute-start(bf16[2,32,2,16,128]{4,3,1,0,2:T(8,128)(2,1)S(1)} %dynamic-slice_bitcast_fusion.1), channel_id=1, source_target_pairs={{0,2},{1,3},{2,0},{3,1},{4,6},{5,7},{6,4},{7,5},{8,10},{9,11},{10,... | collective-permute-start | bytes 1572872 | tf_op jit(solution)/shard_map/ppermute | solution.py:159
  94.3 15.5 %collective-permute-start.8 = (bf16[2,32,16,128]{3,2,1,0:T(8,128)(2,1)S(1)}, bf16[2,32,16,128]{3,2,1,0:T(8,128)(2,1)S(1)}, u32[]{:S(2)}, u32[]{:S(2)}) collective-permute-start(bf16[2,32,16,128]{3,2,1,0:T(8,128)(2,1)S(1)} %dynamic-slice_bitcast_fusion.2), channel_id=1, source_target_pairs={{0,4},{1,5},{2,6},{3,7},{4,0},{5,1},{6,2},{7,3},{8,12},{9,13},{10,... | collective-permute-start | bytes 786440 | tf_op jit(solution)/shard_map/ppermute | solution.py:159
